TPU v7x, 256 devices: a whole 4x4x8 slice. The times are simulated.
256 devices in a mesh: dp: 32 (over z, y), ep: 8 (over x, core).
Axes of the slice: x: 4, y: 4, z: 8, core: 2. Of those that a mesh axis runs over, the one named last changes fastest.
Arguments:
- states: bfloat16 [2048, 16, 128, 128], P(('dp', 'ep')), may hold values from -4 to 4
- query_rows: bfloat16 [2048, 4, 1024], P(('dp', 'ep')), may hold values from -6 to 6
- key_rows: bfloat16 [2048, 4, 1024], P(('dp', 'ep')), may hold values from -6 to 6
- value_rows: bfloat16 [2048, 4, 2048], P(('dp', 'ep')), may hold values from -6 to 6
- gate_rows: bfloat16 [2048, 4, 2048], P(('dp', 'ep')), may hold values from -6 to 6
- beta_logit: bfloat16 [2048, 4, 16], P(('dp', 'ep')), may hold values from -6 to 6
- decay_logit: bfloat16 [2048, 4, 16], P(('dp', 'ep')), may hold values from -8 to 8
- residual: bfloat16 [2048, 4, 2048], P(('dp', 'ep')), may hold values from -6 to 6
- route_ids: int32 [2048, 4, 10], P(('dp', 'ep')), may hold values from 0 to 255, all different within a row; in each aligned block of 32 rows (0 to 31, 32 to 63, ..., all dimensions but the last counted through in order) at most 3 rows name the same one
- route_prob: float32 [2048, 4, 10], P(('dp', 'ep')), may hold values from 0.05 to 1
- out_weight: bfloat16 [2048, 2048], P(None, 'ep'), may hold values from -0.125 to 0.125
- core_gain: float32 [128], replicated, may hold values from 0.1 to 1.9
- moe_gain: float32 [2048], replicated, may hold values from 0.1 to 1.9
- gate_up: bfloat16 [256, 2048, 512], P(('dp', 'ep')), may hold values from -0.125 to 0.125
- down_weight: bfloat16 [256, 256, 2048], P(('dp', 'ep')), may hold values from -0.375 to 0.375
- new_home: int32 [2048], P(('dp', 'ep')), may hold values from 0 to 2047, as said below
Outputs:
- mixed_out: bfloat16 [2048, 4, 2048], P(('dp', 'ep'))
- moved_out: bfloat16 [2048, 16, 128, 128], P(('dp', 'ep'))
Inputs may be any that keep to these rules, and one draw needn't show every extreme that they name: `route_ids`: each row names 10 different experts; among the 32 rows of one device (its requests, each with its 4 tokens) no expert is named more than 3 times, a bound that some block reaches. `new_home`: A permutation of the request positions; a request stays among the 8 devices of its dp index, and every device hands exactly 1 of its requests to each device of that group, itself included.
All inputs are finite; a program needn't handle non-finite values.
Results may differ from a plain program's by a relative error of at most 0.01.
Values may be sent and summed in bfloat16 or wider, within the bound.
A program may use at most 128 MiB of HBM per device.

v0:
```python
import jax
import jax.numpy as jnp
from jax import lax
from jax.sharding import PartitionSpec as P

epsilon = 1e-06


def unit_rows(values):
    return values * lax.rsqrt(jnp.sum(values * values, -1, keepdims=True) + epsilon)


def delta_block(
    state_in, query_rows, key_rows, value_rows, gate_rows, beta_logit, decay_logit, core_gain
):
    batch_size = state_in.shape[0]
    head_count = decay_logit.shape[-1]
    head_width = state_in.shape[-1]
    key_heads = query_rows.shape[-1] // head_width
    repeats = head_count // key_heads
    memory_state = state_in.astype(jnp.float32)
    outputs = []
    for position in range(query_rows.shape[1]):
        queries = unit_rows(
            query_rows[:, position].astype(jnp.float32).reshape(batch_size, key_heads, head_width)
        )
        queries = jnp.repeat(queries, repeats, axis=1) * head_width ** (-0.5)
        key_units = unit_rows(
            key_rows[:, position].astype(jnp.float32).reshape(batch_size, key_heads, head_width)
        )
        key_units = jnp.repeat(key_units, repeats, axis=1)
        values = (
            value_rows[:, position].astype(jnp.float32).reshape(batch_size, head_count, head_width)
        )
        decays = jax.nn.sigmoid(decay_logit[:, position].astype(jnp.float32))
        strength = jax.nn.sigmoid(beta_logit[:, position].astype(jnp.float32))
        memory_state = memory_state * decays[:, :, None, None]
        memory = jnp.einsum(
            "bhkv,bhk->bhv", memory_state, key_units, precision=lax.Precision.HIGHEST
        )
        update = (values - memory) * strength[:, :, None]
        memory_state = memory_state + key_units[:, :, :, None] * update[:, :, None, :]
        reading = jnp.einsum(
            "bhkv,bhk->bhv", memory_state, queries, precision=lax.Precision.HIGHEST
        )
        scaled = reading * lax.rsqrt(jnp.mean(reading * reading, -1, keepdims=True) + epsilon)
        gate_vals = (
            gate_rows[:, position].astype(jnp.float32).reshape(batch_size, head_count, head_width)
        )
        gated_out = scaled * core_gain * jax.nn.silu(gate_vals)
        outputs.append(gated_out.reshape(batch_size, head_count * head_width).astype(jnp.bfloat16))
    return (memory_state.astype(jnp.bfloat16), jnp.stack(outputs, axis=1))


def rms_scale(values, gain):
    return values * lax.rsqrt(jnp.mean(values * values, -1, keepdims=True) + epsilon) * gain


def expert_apply(chosen_rows, gate_up, down_weight):
    hidden_units = down_weight.shape[0]
    joined = jnp.dot(chosen_rows, gate_up, preferred_element_type=jnp.float32)
    active = (jax.nn.silu(joined[:, :hidden_units]) * joined[:, hidden_units:]).astype(jnp.bfloat16)
    return jnp.dot(active, down_weight, preferred_element_type=jnp.float32).astype(jnp.bfloat16)


def pack(values, positions, lane_count):
    zeroed = jnp.zeros(values.shape, values.dtype)
    placed = zeroed.at[positions].set(values)
    return placed.reshape((lane_count, values.shape[0] // lane_count) + values.shape[1:])


def unpack(values):
    return values.reshape((values.shape[0] * values.shape[1],) + values.shape[2:])


def shards(
    states,
    query_rows,
    key_rows,
    value_rows,
    gate_rows,
    beta_logit,
    decay_logit,
    residual,
    route_ids,
    route_prob,
    out_weight,
    core_gain,
    moe_gain,
    gate_up,
    down_weight,
    new_home,
):
    req_count = states.shape[0]
    step_count = query_rows.shape[1]
    model_width = residual.shape[-1]
    ep_size = lax.axis_size("ep")
    dp_size = lax.axis_size("dp")
    target = new_home // req_count % ep_size
    new_place = new_home % req_count
    order_ids = jnp.arange(req_count, dtype=jnp.int32)
    earlier = (target[:, None] == target[None, :]) & (order_ids[None, :] < order_ids[:, None])
    lane_rank = jnp.sum(earlier.astype(jnp.int32), axis=1)
    lane_cap = req_count // ep_size
    buffer_index = target * lane_cap + lane_rank
    fresh_states, core_out = delta_block(
        states, query_rows, key_rows, value_rows, gate_rows, beta_logit, decay_logit, core_gain
    )
    received = (
        lax.all_to_all(
            pack(fresh_states, buffer_index, ep_size), "ep", split_axis=0, concat_axis=0, tiled=True
        ),
        lax.all_to_all(
            pack(new_place, buffer_index, ep_size), "ep", split_axis=0, concat_axis=0, tiled=True
        ),
    )
    moved_out = jnp.zeros_like(states).at[unpack(received[1])].set(unpack(received[0]), mode="drop")
    token_count = req_count * step_count
    core_flat = core_out.reshape(token_count, core_out.shape[-1])
    columns = jnp.dot(
        lax.all_gather(core_flat, "ep", axis=0, tiled=True),
        out_weight,
        preferred_element_type=jnp.float32,
    ).astype(jnp.bfloat16)
    attention = lax.all_to_all(columns, "ep", split_axis=0, concat_axis=1, tiled=True)
    hidden = (
        residual.reshape(token_count, model_width).astype(jnp.float32)
        + attention.astype(jnp.float32)
    ).astype(jnp.bfloat16)
    normed = rms_scale(hidden.astype(jnp.float32), moe_gain).astype(jnp.bfloat16)
    top_count = route_ids.shape[-1]
    experts = dp_size * ep_size
    capacity = (token_count * top_count + experts - 1) // experts + 1
    flat_ids = route_ids.reshape(-1)
    onehot = (flat_ids[:, None] == jnp.arange(experts, dtype=jnp.int32)[None, :]).astype(jnp.int32)
    route_rank = jnp.sum(jnp.cumsum(onehot, axis=0) * onehot, axis=1) - 1
    slot_index = flat_ids * capacity + route_rank
    outgoing = (
        jnp.zeros((experts * capacity, model_width), jnp.bfloat16)
        .at[slot_index]
        .set(jnp.repeat(normed, top_count, axis=0))
    )
    arrived = lax.all_to_all(
        lax.all_to_all(
            outgoing.reshape(dp_size, ep_size, capacity, model_width),
            "dp",
            split_axis=0,
            concat_axis=0,
            tiled=True,
        ),
        "ep",
        split_axis=1,
        concat_axis=1,
        tiled=True,
    )
    result = expert_apply(arrived.reshape(-1, model_width), gate_up[0], down_weight[0]).reshape(
        dp_size, ep_size, capacity, model_width
    )
    returned = lax.all_to_all(
        lax.all_to_all(result, "dp", split_axis=0, concat_axis=0, tiled=True),
        "ep",
        split_axis=1,
        concat_axis=1,
        tiled=True,
    )
    routed = returned.reshape(experts * capacity, model_width)[slot_index]
    weights = route_prob.reshape(token_count, top_count)
    weights = weights / jnp.sum(weights, -1, keepdims=True)
    combined = jnp.sum(
        routed.reshape(token_count, top_count, model_width).astype(jnp.float32)
        * weights[:, :, None],
        axis=1,
    )
    mixed_out = (
        (hidden.astype(jnp.float32) + combined)
        .astype(jnp.bfloat16)
        .reshape(req_count, step_count, model_width)
    )
    return (mixed_out, moved_out)


def solution(mesh):
    placed = (
        P(("dp", "ep"), None, None, None),
        P(("dp", "ep"), None, None),
        P(("dp", "ep"), None, None),
        P(("dp", "ep"), None, None),
        P(("dp", "ep"), None, None),
        P(("dp", "ep"), None, None),
        P(("dp", "ep"), None, None),
        P(("dp", "ep"), None, None),
        P(("dp", "ep"), None, None),
        P(("dp", "ep"), None, None),
        P(None, "ep"),
        P(),
        P(),
        P(("dp", "ep"), None, None),
        P(("dp", "ep"), None, None),
        P(("dp", "ep")),
    )
    return jax.shard_map(
        shards,
        mesh=mesh,
        in_specs=placed,
        out_specs=(P(("dp", "ep"), None, None), P(("dp", "ep"), None, None, None)),
        check_vma=False,
    )
```

profile of v0, /device:TPU:24, one launch (start us, length us, event | category | flops | bytes accessed | tf_op | source)
XLA Modules:
  0.0 571.1 jit_solution(461292190551067246)
XLA Ops:
  14.3 9.7 %fusion = f32[8,16,1,128]{3,2,1,0:T(1,128)S(1)} fusion(f32[8,16,128,1]{2,3,1,0:T(1,128)S(1)} %bitcast.152, bf16[8,16,128,128]{3,2,1,0:T(8,128)(2,1)} %param.16, f32[8,16]{1,0:T(8,128)S(1)} %get-tuple-element.37), kind=kOutput, calls=%fused_computation.10 | convolution fusion | flops 29360128 | bytes 4325888 | tf_op jit(solution)/shard_map/bhkv,bhk->bhv/dot_general | solution.py:38
  24.1 8.3 %fusion.2 = f32[8,16,1,128]{3,2,1,0:T(1,128)S(1)} fusion(f32[8,16,128,1]{2,3,1,0:T(1,128)S(1)} %bitcast.196, bf16[8,16,128,128]{3,2,1,0:T(8,128)(2,1)S(1)} %copy-done.1, f32[8,16,128]{2,1,0:T(8,128)S(1)} %subtract_multiply_fusion.3, f32[8,16,128]{2,1,0:T(8,128)S(1)} %bitcast.153, f32[8,16]{1,0:T(8,128)S(1)} %get-tuple-element.37), kind=kOutput, calls=%fused_computation.12 | convolution fusion | flops 33554432 | bytes 4456960 | tf_op jit(solution)/shard_map/bhkv,bhk->bhv/dot_general | solution.py:43
  32.6 9.0 %fusion.3 = f32[8,16,1,128]{3,2,1,0:T(1,128)S(1)} fusion(f32[8,16,128,1]{2,3,1,0:T(1,128)S(1)} %bitcast.161, bf16[8,16,128,128]{3,2,1,0:T(8,128)(2,1)S(1)} %copy-done.1, f32[8,16]{1,0:T(8,128)S(1)} %get-tuple-element.36, f32[8,16,128]{2,1,0:T(8,128)S(1)} %subtract_multiply_fusion.3, f32[8,16,128]{2,1,0:T(8,128)S(1)} %bitcast.154, ...), kind=kOutput, calls=%fused_computation.13 | convolution fusion | flops 35651584 | bytes 4457472 | tf_op jit(solution)/shard_map/bhkv,bhk->bhv/dot_general | solution.py:38
  41.7 11.6 %fusion.11 = f32[8,16,1,128]{3,2,1,0:T(1,128)S(1)} fusion(f32[8,16,128,1]{2,3,1,0:T(1,128)S(1)} %bitcast.197, bf16[8,16,128,128]{3,2,1,0:T(8,128)(2,1)S(1)} %copy-done.1, f32[8,16,128]{2,1,0:T(8,128)S(1)} %subtract_multiply_fusion.2, f32[8,16,128]{2,1,0:T(8,128)S(1)} %bitcast.162, f32[8,16]{1,0:T(8,128)S(1)} %get-tuple-element.36, ...), kind=kOutput, calls=%fused_computation.20 | convolution fusion | flops 39845888 | bytes 4588544 | tf_op jit(solution)/shard_map/bhkv,bhk->bhv/dot_general | solution.py:43
  53.4 11.7 %fusion.7 = f32[8,16,1,128]{3,2,1,0:T(1,128)S(1)} fusion(f32[8,16,128,1]{2,3,1,0:T(1,128)S(1)} %bitcast.168, bf16[8,16,128,128]{3,2,1,0:T(8,128)(2,1)S(1)} %copy-done.1, f32[8,16]{1,0:T(8,128)S(1)} %get-tuple-element.35, f32[8,16,128]{2,1,0:T(8,128)S(1)} %subtract_multiply_fusion.2, f32[8,16,128]{2,1,0:T(8,128)S(1)} %bitcast.163, ...), kind=kOutput, calls=%fused_computation.16 | convolution fusion | flops 41943040 | bytes 4589056 | tf_op jit(solution)/shard_map/bhkv,bhk->bhv/dot_general | solution.py:38
  65.2 15.5 %fusion.43 = f32[8,16,1,128]{3,2,1,0:T(1,128)S(1)} fusion(f32[8,16,128,1]{2,3,1,0:T(1,128)S(1)} %bitcast.198, bf16[8,16,128,128]{3,2,1,0:T(8,128)(2,1)S(1)} %copy-done.1, f32[8,16,128]{2,1,0:T(8,128)S(1)} %subtract_multiply_fusion.1, f32[8,16,128]{2,1,0:T(8,128)S(1)} %bitcast.169, f32[8,16]{1,0:T(8,128)S(1)} %get-tuple-element.35, ...), kind=kOutput, calls=%fused_computation.56 | convolution fusion | flops 46137344 | bytes 4720128 | tf_op jit(solution)/shard_map/bhkv,bhk->bhv/dot_general | solution.py:43
  80.9 15.6 %fusion.5 = f32[8,16,1,128]{3,2,1,0:T(1,128)S(1)} fusion(f32[8,16,128,1]{2,3,1,0:T(1,128)S(1)} %bitcast.173, f32[8,16]{1,0:T(8,128)S(1)} %get-tuple-element.34, bf16[8,16,128,128]{3,2,1,0:T(8,128)(2,1)S(1)} %copy-done.1, f32[8,16,128]{2,1,0:T(8,128)S(1)} %subtract_multiply_fusion.1, f32[8,16,128]{2,1,0:T(8,128)S(1)} %bitcast.170, ...), kind=kOutput, calls=%fused_computation.14 | convolution fusion | flops 48234496 | bytes 4720640 | tf_op jit(solution)/shard_map/bhkv,bhk->bhv/dot_general | solution.py:38
  96.8 21.1 %fusion.10 = f32[8,16,1,128]{3,2,1,0:T(1,128)S(1)} fusion(f32[8,16,128,1]{2,3,1,0:T(1,128)S(1)} %bitcast.199, f32[8,16,128]{2,1,0:T(8,128)S(1)} %subtract_multiply_fusion, f32[8,16,128]{2,1,0:T(8,128)S(1)} %bitcast.174, f32[8,16]{1,0:T(8,128)S(1)} %get-tuple-element.34, bf16[8,16,128,128]{3,2,1,0:T(8,128)(2,1)S(1)} %copy-done.1, ...), kind=kOutput, calls=%fused_computation.19 | convolution fusion | flops 52428800 | bytes 4851712 | tf_op jit(solution)/shard_map/bhkv,bhk->bhv/dot_general | solution.py:43
  120.4 27.7 %all-gather.2.cloned.1.call-done = bf16[256,2048]{1,0:T(8,128)(2,1)} async-done(((bf16[32,2048]{1,0:T(8,128)(2,1)}), bf16[256,2048]{1,0:T(8,128)(2,1)}) %all-gather.2.cloned.1.call-update) | async-done | bytes 1048592 | tf_op jit(solution)/shard_map/all_gather | solution.py:121
  155.1 5.3 all-to-all-done
  166.9 5.4 scatter_custom_fusion
  172.3 9.1 %reshape.504 = bf16[32,8,3,2048]{3,2,1,0:T(4,128)(2,1)} reshape(bf16[768,2048]{1,0:T(8,128)(2,1)} %scatter_custom_fusion) | data formatting | bytes 6291456 | tf_op jit(solution)/shard_map/reshape | solution.py:145
  181.4 5.5 copy.104
  186.9 82.7 %all_to_all.50 = bf16[32,8,3,2048]{3,1,2,0:T(8,128)(2,1)S(1)} all-to-all(bf16[32,8,3,2048]{3,1,2,0:T(8,128)(2,1)S(1)} %copy.104), channel_id=1, replica_groups=mesh['dp'=32,'ep'=8] {'dp'}, dimensions={0} | all-to-all | bytes 6291456 | tf_op jit(solution)/shard_map/all_to_all | solution.py:144
  273.1 4.6 all-to-all-start.2
  279.1 36.9 %all-to-all-done.2 = bf16[32,8,3,2048]{3,0,2,1:T(8,128)(2,1)} async-done(((bf16[32,8,3,2048]{3,0,2,1:T(8,128)(2,1)}), bf16[32,8,3,2048]{3,0,2,1:T(8,128)(2,1)}, u32[]{:S(2)}, u32[]{:S(2)}) %all-to-all-start.2) | async-done | bytes 3145760 | tf_op jit(solution)/shard_map/all_to_all | solution.py:143
  319.6 6.6 %copy.106 = bf16[32,8,3,2048]{3,2,1,0:T(4,128)(2,1)} copy(bf16[32,8,3,2048]{3,0,2,1:T(8,128)(2,1)} %all-to-all-done.2) | data formatting | bytes 6291456 | tf_op jit(solution)/shard_map/all_to_all | solution.py:143
  326.2 8.8 %reshape.505 = bf16[768,2048]{1,0:T(8,128)(2,1)} reshape(bf16[32,8,3,2048]{3,2,1,0:T(4,128)(2,1)} %copy.106) | data formatting | bytes 6291456 | tf_op jit(solution)/shard_map/reshape | solution.py:156
  341.5 9.1 %reshape.506 = bf16[32,8,3,2048]{3,2,1,0:T(4,128)(2,1)} reshape(bf16[768,2048]{1,0:T(8,128)(2,1)} %convolution_convert_fusion) | data formatting | bytes 6291456 | tf_op jit(solution)/shard_map/reshape | solution.py:156
  350.6 7.2 %copy.107 = bf16[32,8,3,2048]{3,1,2,0:T(8,128)(2,1)} copy(bf16[32,8,3,2048]{3,2,1,0:T(4,128)(2,1)} %reshape.506) | data formatting | bytes 6291456 | tf_op jit(solution)/shard_map/reshape | solution.py:156
  357.9 5.8 %all-to-all-start.3 = ((bf16[32,8,3,2048]{3,1,2,0:T(8,128)(2,1)}), bf16[32,8,3,2048]{3,1,2,0:T(8,128)(2,1)}, u32[]{:S(2)}, u32[]{:S(2)}) async-start(bf16[32,8,3,2048]{3,1,2,0:T(8,128)(2,1)} %copy.107), calls=%async_computation.3 | async-start | bytes 6291456 | tf_op jit(solution)/shard_map/all_to_all | solution.py:160
  363.7 13.3 %fusion.9 = bf16[8,16,128,128]{3,2,1,0:T(8,128)(2,1)} fusion(f32[8,16,128]{2,1,0:T(8,128)S(1)} %copy-done.13, f32[8,16,128]{2,1,0:T(8,128)S(1)} %bitcast.175, f32[8,16]{1,0:T(8,128)S(1)} %get-tuple-element.34, f32[8,16,128]{2,1,0:T(8,128)S(1)} %copy-done.11, f32[8,16,128]{2,1,0:T(8,128)S(1)} %bitcast.172, f32[8,16]{1,0:T(8,128)S(1)} %get-tuple-element.35, ...), kind=kLoop, calls=%fused_computation.18 | loop fusion | flops 29360128 | bytes 8914944 | tf_op jit(solution)/shard_map/convert_element_type | solution.py:52
  380.0 10.9 %scatter_fusion = bf16[8,16,128,128]{3,2,1,0:T(8,128)(2,1)} fusion(bf16[8,16,128,128]{3,2,1,0:T(8,128)(2,1)} %broadcast.332.clone, s32[8]{0:T(128)S(1)} %compare_select_fusion.2, bf16[8,16,128,128]{3,2,1,0:T(8,128)(2,1)} %fusion.9), kind=kCustom, calls=%fused_computation.3 | custom fusion | bytes 12582944 | tf_op jit(solution)/shard_map/scatter | solution.py:68
  390.9 46.9 %all-to-all-done.3 = bf16[32,8,3,2048]{3,1,2,0:T(8,128)(2,1)} async-done(((bf16[32,8,3,2048]{3,1,2,0:T(8,128)(2,1)}), bf16[32,8,3,2048]{3,1,2,0:T(8,128)(2,1)}, u32[]{:S(2)}, u32[]{:S(2)}) %all-to-all-start.3) | async-done | bytes 3145760 | tf_op jit(solution)/shard_map/all_to_all | solution.py:160
  437.7 4.8 all-to-all-start.6
  442.5 5.3 copy.108
  447.9 44.3 %all-to-all-done.6 = bf16[8,1,16,128,128]{4,3,2,1,0:T(8,128)(2,1)} async-done(((bf16[8,1,16,128,128]{4,3,2,1,0:T(8,128)(2,1)}), bf16[8,1,16,128,128]{4,3,2,1,0:T(8,128)(2,1)}, u32[]{:S(2)}, u32[]{:S(2)}) %all-to-all-start.6) | async-done | bytes 4194336 | tf_op jit(solution)/shard_map/all_to_all | solution.py:110
  500.8 10.9 %scatter_fusion.1 = bf16[8,16,128,128]{3,2,1,0:T(8,128)(2,1)} fusion(bf16[8,16,128,128]{3,2,1,0:T(8,128)(2,1)} %broadcast.332, s32[8]{0:T(128)S(1)} %fusion.54, bf16[8,16,128,128]{3,2,1,0:T(8,128)(2,1)} %bitcast.77), kind=kCustom, calls=%fused_computation.4 | custom fusion | bytes 12582944 | tf_op jit(solution)/shard_map/scatter | solution.py:117
  511.7 23.4 %all-to-all-done.4 = bf16[32,8,3,2048]{3,0,2,1:T(8,128)(2,1)} async-done(((bf16[32,8,3,2048]{3,0,2,1:T(8,128)(2,1)}), bf16[32,8,3,2048]{3,0,2,1:T(8,128)(2,1)}, u32[]{:S(2)}, u32[]{:S(2)}) %all-to-all-start.4) | async-done | bytes 3145760 | tf_op jit(solution)/shard_map/all_to_all | solution.py:159
  535.1 6.5 %copy.109 = bf16[32,8,3,2048]{3,2,1,0:T(4,128)(2,1)} copy(bf16[32,8,3,2048]{3,0,2,1:T(8,128)(2,1)} %all-to-all-done.4) | data formatting | bytes 6291456 | tf_op jit(solution)/shard_map/all_to_all | solution.py:159
  541.6 8.8 %reshape.507 = bf16[768,2048]{1,0:T(8,128)(2,1)} reshape(bf16[32,8,3,2048]{3,2,1,0:T(4,128)(2,1)} %copy.109) | data formatting | bytes 6291456 | tf_op jit(solution)/shard_map/reshape | solution.py:166
  550.4 6.8 %gather_fusion = bf16[320,2048]{1,0:T(8,128)(2,1)S(1)} fusion(bf16[768,2048]{1,0:T(8,128)(2,1)} %reshape.507, s32[1024]{0:T(1024)} %pad_clamp_fusion), kind=kCustom, calls=%fused_computation | custom fusion | bytes 2622720 | tf_op jit(solution)/shard_map/gather | solution.py:166
  (169 shorter events, 56.7 us)
Async XLA Ops:
  7.2 327.9 %copy-start = (bf16[1,2048,512]{2,1,0:T(8,128)(2,1)S(1)}, bf16[1,2048,512]{2,1,0:T(8,128)(2,1)}, u32[]{:S(2)}) copy-start(bf16[1,2048,512]{2,1,0:T(8,128)(2,1)} %param.29) | copy-start | bytes 6291460
  7.2 140.9 %all-gather.2.cloned.1.call-start = ((), (), s32[]{:S(2)}) async-start(), calls=%async_computation.7 | async-start | bytes 1179648 | tf_op jit(solution)/shard_map/all_gather | solution.py:121
  9.0 15.1 %copy-start.1 = (bf16[8,16,128,128]{3,2,1,0:T(8,128)(2,1)S(1)}, bf16[8,16,128,128]{3,2,1,0:T(8,128)(2,1)}, u32[]{:S(2)}) copy-start(bf16[8,16,128,128]{3,2,1,0:T(8,128)(2,1)} %param.16) | copy-start | bytes 12582916
  14.3 82.4 %copy-start.14 = (f32[8,8,2,128]{3,2,1,0:T(2,128)}, f32[8,8,2,128]{3,2,1,0:T(2,128)S(1)}, u32[]{:S(2)}) copy-start(f32[8,8,2,128]{3,2,1,0:T(2,128)S(1)} %broadcast_in_dim.22) | copy-start | bytes 196612
  24.1 72.6 %copy-start.6 = (f32[8,16,128]{2,1,0:T(8,128)}, f32[8,16,128]{2,1,0:T(8,128)S(1)}, u32[]{:S(2)}) copy-start(f32[8,16,128]{2,1,0:T(8,128)S(1)} %subtract_multiply_fusion.3) | copy-start | bytes 196612
  32.6 64.1 %copy-start.16 = (f32[8,8,2,128]{3,2,1,0:T(2,128)}, f32[8,8,2,128]{3,2,1,0:T(2,128)S(1)}, u32[]{:S(2)}) copy-start(f32[8,8,2,128]{3,2,1,0:T(2,128)S(1)} %broadcast_in_dim.24) | copy-start | bytes 196612
  41.6 55.1 %copy-start.8 = (f32[8,16,128]{2,1,0:T(8,128)}, f32[8,16,128]{2,1,0:T(8,128)S(1)}, u32[]{:S(2)}) copy-start(f32[8,16,128]{2,1,0:T(8,128)S(1)} %subtract_multiply_fusion.2) | copy-start | bytes 196612
  53.4 43.3 %copy-start.18 = (f32[8,8,2,128]{3,2,1,0:T(2,128)}, f32[8,8,2,128]{3,2,1,0:T(2,128)S(1)}, u32[]{:S(2)}) copy-start(f32[8,8,2,128]{3,2,1,0:T(2,128)S(1)} %broadcast_in_dim.26) | copy-start | bytes 196612
  65.2 31.5 %copy-start.10 = (f32[8,16,128]{2,1,0:T(8,128)}, f32[8,16,128]{2,1,0:T(8,128)S(1)}, u32[]{:S(2)}) copy-start(f32[8,16,128]{2,1,0:T(8,128)S(1)} %subtract_multiply_fusion.1) | copy-start | bytes 196612
  80.9 15.8 %copy-start.20 = (f32[8,8,2,128]{3,2,1,0:T(2,128)}, f32[8,8,2,128]{3,2,1,0:T(2,128)S(1)}, u32[]{:S(2)}) copy-start(f32[8,8,2,128]{3,2,1,0:T(2,128)S(1)} %broadcast_in_dim.28) | copy-start | bytes 196612
  96.6 21.3 %copy-start.12 = (f32[8,16,128]{2,1,0:T(8,128)}, f32[8,16,128]{2,1,0:T(8,128)S(1)}, u32[]{:S(2)}) copy-start(f32[8,16,128]{2,1,0:T(8,128)S(1)} %subtract_multiply_fusion) | copy-start | bytes 196612
  96.7 21.3 %copy-start.5 = (bf16[8,4,2048]{2,1,0:T(4,128)(2,1)S(1)}, bf16[8,4,2048]{2,1,0:T(4,128)(2,1)}, u32[]{:S(2)}) copy-start(bf16[8,4,2048]{2,1,0:T(4,128)(2,1)} %param.20) | copy-start | bytes 393220
  96.8 21.5 %copy-start.25 = (f32[128]{0:T(128)S(1)}, f32[128]{0:T(128)}, u32[]{:S(2)}) copy-start(f32[128]{0:T(128)} %param.27) | copy-start | bytes 1540
  96.8 22.6 %copy-start.22 = (s32[8,4,10]{2,1,0:T(4,128)S(1)}, s32[8,4,10]{2,1,0:T(4,128)}, u32[]{:S(2)}) copy-start(s32[8,4,10]{2,1,0:T(4,128)} %param.24) | copy-start | bytes 3844
  118.2 36.2 %copy-start.4 = (bf16[8,4,2048]{2,1,0:T(4,128)(2,1)S(1)}, bf16[8,4,2048]{2,1,0:T(4,128)(2,1)}, u32[]{:S(2)}) copy-start(bf16[8,4,2048]{2,1,0:T(4,128)(2,1)} %param.23) | copy-start | bytes 393220
  150.7 9.6 %all-to-all-start = ((bf16[8,32,256]{2,1,0:T(8,128)(2,1)}), bf16[8,32,256]{2,1,0:T(8,128)(2,1)S(1)}, u32[]{:S(2)}, u32[]{:S(2)}) async-start(bf16[8,32,256]{2,1,0:T(8,128)(2,1)} %bitcast.64), calls=%async_computation | async-start | bytes 262144 | tf_op jit(solution)/shard_map/all_to_all | solution.py:125
  160.7 11.7 %copy-start.2 = (f32[8,4,2048]{2,1,0:T(4,128)}, f32[8,4,2048]{2,1,0:T(4,128)S(1)}, u32[]{:S(2)}) copy-start(f32[8,4,2048]{2,1,0:T(4,128)S(1)} %reshape.543) | copy-start | bytes 786436
  273.1 43.0 %all-to-all-start.2 = ((bf16[32,8,3,2048]{3,0,2,1:T(8,128)(2,1)}), bf16[32,8,3,2048]{3,0,2,1:T(8,128)(2,1)}, u32[]{:S(2)}, u32[]{:S(2)}) async-start(bf16[32,8,3,2048]{3,0,2,1:T(8,128)(2,1)} %copy.105), calls=%async_computation.2 | async-start | bytes 6291456 | tf_op jit(solution)/shard_map/all_to_all | solution.py:143
  316.1 41.8 %all-to-all-start.5 = ((s32[8,1,1]{2,1,0:T(1,128)}), s32[8,1,1]{2,1,0:T(1,128)S(1)}, u32[]{:S(2)}, u32[]{:S(2)}) async-start(s32[8,1,1]{2,1,0:T(1,128)} %copy.110), calls=%async_computation.5 | async-start | bytes 8192 | tf_op jit(solution)/shard_map/all_to_all | solution.py:113
  357.8 5.8 %copy-start.7 = (f32[8,16,128]{2,1,0:T(8,128)S(1)}, f32[8,16,128]{2,1,0:T(8,128)}, u32[]{:S(2)}) copy-start(f32[8,16,128]{2,1,0:T(8,128)} %copy-done.6) | copy-start | bytes 196612
  357.8 5.8 %copy-start.9 = (f32[8,16,128]{2,1,0:T(8,128)S(1)}, f32[8,16,128]{2,1,0:T(8,128)}, u32[]{:S(2)}) copy-start(f32[8,16,128]{2,1,0:T(8,128)} %copy-done.8) | copy-start | bytes 196612
  357.8 5.8 %copy-start.11 = (f32[8,16,128]{2,1,0:T(8,128)S(1)}, f32[8,16,128]{2,1,0:T(8,128)}, u32[]{:S(2)}) copy-start(f32[8,16,128]{2,1,0:T(8,128)} %copy-done.10) | copy-start | bytes 196612
  357.8 5.9 %copy-start.13 = (f32[8,16,128]{2,1,0:T(8,128)S(1)}, f32[8,16,128]{2,1,0:T(8,128)}, u32[]{:S(2)}) copy-start(f32[8,16,128]{2,1,0:T(8,128)} %copy-done.12) | copy-start | bytes 196612
  357.8 5.9 %copy-start.15 = (f32[8,8,2,128]{3,2,1,0:T(2,128)S(1)}, f32[8,8,2,128]{3,2,1,0:T(2,128)}, u32[]{:S(2)}) copy-start(f32[8,8,2,128]{3,2,1,0:T(2,128)} %copy-done.14) | copy-start | bytes 196612
  357.8 5.9 %copy-start.17 = (f32[8,8,2,128]{3,2,1,0:T(2,128)S(1)}, f32[8,8,2,128]{3,2,1,0:T(2,128)}, u32[]{:S(2)}) copy-start(f32[8,8,2,128]{3,2,1,0:T(2,128)} %copy-done.16) | copy-start | bytes 196612
  357.8 5.9 %copy-start.19 = (f32[8,8,2,128]{3,2,1,0:T(2,128)S(1)}, f32[8,8,2,128]{3,2,1,0:T(2,128)}, u32[]{:S(2)}) copy-start(f32[8,8,2,128]{3,2,1,0:T(2,128)} %copy-done.18) | copy-start | bytes 196612
  357.8 5.9 %copy-start.21 = (f32[8,8,2,128]{3,2,1,0:T(2,128)S(1)}, f32[8,8,2,128]{3,2,1,0:T(2,128)}, u32[]{:S(2)}) copy-start(f32[8,8,2,128]{3,2,1,0:T(2,128)} %copy-done.20) | copy-start | bytes 196612
  357.9 79.9 %all-to-all-start.3 = ((bf16[32,8,3,2048]{3,1,2,0:T(8,128)(2,1)}), bf16[32,8,3,2048]{3,1,2,0:T(8,128)(2,1)}, u32[]{:S(2)}, u32[]{:S(2)}) async-start(bf16[32,8,3,2048]{3,1,2,0:T(8,128)(2,1)} %copy.107), calls=%async_computation.3 | async-start | bytes 6291456 | tf_op jit(solution)/shard_map/all_to_all | solution.py:160
  437.7 54.5 %all-to-all-start.6 = ((bf16[8,1,16,128,128]{4,3,2,1,0:T(8,128)(2,1)}), bf16[8,1,16,128,128]{4,3,2,1,0:T(8,128)(2,1)}, u32[]{:S(2)}, u32[]{:S(2)}) async-start(bf16[8,1,16,128,128]{4,3,2,1,0:T(8,128)(2,1)} %bitcast.132), calls=%async_computation.6 | async-start | bytes 8388608 | tf_op jit(solution)/shard_map/all_to_all | solution.py:110
  447.9 48.8 %copy-start.23 = (f32[8,4,10]{2,1,0:T(4,128)S(1)}, f32[8,4,10]{2,1,0:T(4,128)}, u32[]{:S(2)}) copy-start(f32[8,4,10]{2,1,0:T(4,128)} %param.25) | copy-start | bytes 3844
  447.9 49.0 %copy-start.24 = (s32[320]{0:T(512)S(1)}, s32[320]{0:T(512)}, u32[]{:S(2)}) copy-start(s32[320]{0:T(512)} %fusion.52) | copy-start | bytes 3844
  492.2 42.9 %all-to-all-start.4 = ((bf16[32,8,3,2048]{3,0,2,1:T(8,128)(2,1)}), bf16[32,8,3,2048]{3,0,2,1:T(8,128)(2,1)}, u32[]{:S(2)}, u32[]{:S(2)}) async-start(bf16[32,8,3,2048]{3,0,2,1:T(8,128)(2,1)} %copy.108), calls=%async_computation.4 | async-start | bytes 6291456 | tf_op jit(solution)/shard_map/all_to_all | solution.py:159
  (3 other events, 12.1 us)
Sparse Core Ops, SparseCore 0:
  119.5 28.5 all-gather.1
where the time goes:
time: 577 us; the launch traced here: 571 us
  waiting for transfers between devices  185 us (32%)
  local copies, waits for them, and re-layouts  123 us (21%)
  matrix products  112 us (19%)
  blocking collectives  82.7 us (14%)
  other arithmetic  27.5 us (5%)
  starting transfers between devices  26.7 us (5%)
  between operations  15.4 us (3%)
    all_to_all x1, blocking collectives, shards(): lax.all_to_all(outgoing.reshape(dp_size, ep_size, capacity, model_width),...  82.7 us
    dot_general x4, matrix products, delta_block(): jnp.einsum('bhkv,bhk->bhv', memory_state, queries, precision=lax.Precisio...  56.5 us
    all_to_all x1, waiting for transfers between devices, shards(): lax.all_to_all(result, 'dp', split_axis=0, concat_axis=0, tiled=True)  46.9 us
    dot_general x4, matrix products, delta_block(): jnp.einsum('bhkv,bhk->bhv', memory_state, key_units, precision=lax.Precis...  45.9 us
    all_to_all x1, waiting for transfers between devices, shards(): lax.all_to_all(pack(fresh_states, buffer_index, ep_size), 'ep', split_axi...  44.3 us
    all_to_all x1, waiting for transfers between devices, shards(): lax.all_to_all(lax.all_to_all(outgoing.reshape(dp_size, ep_size, capacity...  36.9 us
    all_gather x1, waiting for transfers between devices, shards(): lax.all_gather(core_flat, 'ep', axis=0, tiled=True)  27.7 us
    all_to_all x1, waiting for transfers between devices, shards(): lax.all_to_all(lax.all_to_all(result, 'dp', split_axis=0, concat_axis=0,...  23.4 us
  transfers between devices with their start and end apart: 7, of which 6 were waited for; matrix products, arithmetic and copies ran while one was open for 16% of the time, Pallas kernels for 0%

commit v1 on v0

--- a/solution.py
+++ b/solution.py
@@ -4,6 +4,14 @@
 from jax.sharding import PartitionSpec as P
 
 epsilon = 1e-06
+
+
+def rest_lanes(work_x, group_axis):
+    full_n = lax.axis_size(group_axis)
+    ledger = list(map(lambda no: full_n if no == 0 else 1, range(work_x.ndim)))
+    return lax.all_to_all(
+        jnp.tile(work_x, ledger), group_axis, split_axis=0, concat_axis=0, tiled=True
+    )
 
 
 def unit_rows(values):
@@ -118,9 +126,7 @@
     token_count = req_count * step_count
     core_flat = core_out.reshape(token_count, core_out.shape[-1])
     columns = jnp.dot(
-        lax.all_gather(core_flat, "ep", axis=0, tiled=True),
-        out_weight,
-        preferred_element_type=jnp.float32,
+        rest_lanes(core_flat, group_axis="ep"), out_weight, preferred_element_type=jnp.float32
     ).astype(jnp.bfloat16)
     attention = lax.all_to_all(columns, "ep", split_axis=0, concat_axis=1, tiled=True)
     hidden = (

time: 577 us -> 557 us (0.965)
  waiting for transfers between devices: 185 us -> 170 us
  between operations: 15.4 us -> 1.99 us
    all_gather x1 -> x0, waiting for transfers between devices: 27.7 us -> none  [shards(): lax.all_gather(core_flat, 'ep', axis=0, tiled=True)]
    all_to_all x0 -> x1, waiting for transfers between devices: none -> 13.1 us  [rest_lanes(): lax.all_to_all(jnp.tile(work_x, ledger), group_axis, split_axis=0, concat...]
where the time goes in v1:
time: 557 us; the launch traced here: 551 us
  waiting for transfers between devices  170 us (31%)
  local copies, waits for them, and re-layouts  124 us (22%)
  matrix products  111 us (20%)
  blocking collectives  84.1 us (15%)
  starting transfers between devices  31.1 us (6%)
  other arithmetic  28.5 us (5%)
    all_to_all x1, blocking collectives, shards(): lax.all_to_all(outgoing.reshape(dp_size, ep_size, capacity, model_width),...  84.1 us
    dot_general x4, matrix products, delta_block(): jnp.einsum('bhkv,bhk->bhv', memory_state, queries, precision=lax.Precisio...  56.5 us
    all_to_all x1, waiting for transfers between devices, shards(): lax.all_to_all(result, 'dp', split_axis=0, concat_axis=0, tiled=True)  46.9 us
    dot_general x4, matrix products, delta_block(): jnp.einsum('bhkv,bhk->bhv', memory_state, key_units, precision=lax.Precis...  45.9 us
    all_to_all x1, waiting for transfers between devices, shards(): lax.all_to_all(pack(fresh_states, buffer_index, ep_size), 'ep', split_axi...  44.3 us
    all_to_all x1, waiting for transfers between devices, shards(): lax.all_to_all(lax.all_to_all(outgoing.reshape(dp_size, ep_size, capacity...  36.9 us
    all_to_all x1, waiting for transfers between devices, shards(): lax.all_to_all(lax.all_to_all(result, 'dp', split_axis=0, concat_axis=0,...  23.4 us
    reshape x2, local copies, waits for them, and re-layouts, shards(): expert_apply(arrived.reshape(-1, model_width), gate_up[0], down_weight[0])  16.3 us
  transfers between devices with their start and end apart: 7, of which 6 were waited for; matrix products, arithmetic and copies ran while one was open for 16% of the time, Pallas kernels for 0%

profile of v1, /device:TPU:24, one launch (start us, length us, event | category | flops | bytes accessed | tf_op | source)
XLA Modules:
  0.0 550.8 jit_solution(10348469416959453216)
XLA Ops:
  7.7 9.7 %fusion = f32[8,16,1,128]{3,2,1,0:T(1,128)S(1)} fusion(f32[8,16,128,1]{2,3,1,0:T(1,128)S(1)} %bitcast.154, bf16[8,16,128,128]{3,2,1,0:T(8,128)(2,1)} %param.16, f32[8,16]{1,0:T(8,128)S(1)} %get-tuple-element.37), kind=kOutput, calls=%fused_computation.10 | convolution fusion | flops 29360128 | bytes 4325888 | tf_op jit(solution)/shard_map/bhkv,bhk->bhv/dot_general | solution.py:46
  17.6 8.3 %fusion.2 = f32[8,16,1,128]{3,2,1,0:T(1,128)S(1)} fusion(f32[8,16,128,1]{2,3,1,0:T(1,128)S(1)} %bitcast.198, bf16[8,16,128,128]{3,2,1,0:T(8,128)(2,1)S(1)} %copy-done.1, f32[8,16,128]{2,1,0:T(8,128)S(1)} %subtract_multiply_fusion.3, f32[8,16,128]{2,1,0:T(8,128)S(1)} %bitcast.155, f32[8,16]{1,0:T(8,128)S(1)} %get-tuple-element.37), kind=kOutput, calls=%fused_computation.12 | convolution fusion | flops 33554432 | bytes 4456960 | tf_op jit(solution)/shard_map/bhkv,bhk->bhv/dot_general | solution.py:51
  26.0 9.0 %fusion.3 = f32[8,16,1,128]{3,2,1,0:T(1,128)S(1)} fusion(f32[8,16,128,1]{2,3,1,0:T(1,128)S(1)} %bitcast.163, bf16[8,16,128,128]{3,2,1,0:T(8,128)(2,1)S(1)} %copy-done.1, f32[8,16]{1,0:T(8,128)S(1)} %get-tuple-element.36, f32[8,16,128]{2,1,0:T(8,128)S(1)} %subtract_multiply_fusion.3, f32[8,16,128]{2,1,0:T(8,128)S(1)} %bitcast.156, ...), kind=kOutput, calls=%fused_computation.13 | convolution fusion | flops 35651584 | bytes 4457472 | tf_op jit(solution)/shard_map/bhkv,bhk->bhv/dot_general | solution.py:46
  35.1 11.6 %fusion.11 = f32[8,16,1,128]{3,2,1,0:T(1,128)S(1)} fusion(f32[8,16,128,1]{2,3,1,0:T(1,128)S(1)} %bitcast.199, bf16[8,16,128,128]{3,2,1,0:T(8,128)(2,1)S(1)} %copy-done.1, f32[8,16,128]{2,1,0:T(8,128)S(1)} %subtract_multiply_fusion.2, f32[8,16,128]{2,1,0:T(8,128)S(1)} %bitcast.164, f32[8,16]{1,0:T(8,128)S(1)} %get-tuple-element.36, ...), kind=kOutput, calls=%fused_computation.20 | convolution fusion | flops 39845888 | bytes 4588544 | tf_op jit(solution)/shard_map/bhkv,bhk->bhv/dot_general | solution.py:51
  46.9 11.7 %fusion.7 = f32[8,16,1,128]{3,2,1,0:T(1,128)S(1)} fusion(f32[8,16,128,1]{2,3,1,0:T(1,128)S(1)} %bitcast.170, bf16[8,16,128,128]{3,2,1,0:T(8,128)(2,1)S(1)} %copy-done.1, f32[8,16]{1,0:T(8,128)S(1)} %get-tuple-element.35, f32[8,16,128]{2,1,0:T(8,128)S(1)} %subtract_multiply_fusion.2, f32[8,16,128]{2,1,0:T(8,128)S(1)} %bitcast.165, ...), kind=kOutput, calls=%fused_computation.16 | convolution fusion | flops 41943040 | bytes 4589056 | tf_op jit(solution)/shard_map/bhkv,bhk->bhv/dot_general | solution.py:46
  58.7 15.5 %fusion.43 = f32[8,16,1,128]{3,2,1,0:T(1,128)S(1)} fusion(f32[8,16,128,1]{2,3,1,0:T(1,128)S(1)} %bitcast.200, bf16[8,16,128,128]{3,2,1,0:T(8,128)(2,1)S(1)} %copy-done.1, f32[8,16,128]{2,1,0:T(8,128)S(1)} %subtract_multiply_fusion.1, f32[8,16,128]{2,1,0:T(8,128)S(1)} %bitcast.171, f32[8,16]{1,0:T(8,128)S(1)} %get-tuple-element.35, ...), kind=kOutput, calls=%fused_computation.56 | convolution fusion | flops 46137344 | bytes 4720128 | tf_op jit(solution)/shard_map/bhkv,bhk->bhv/dot_general | solution.py:51
  74.3 15.6 %fusion.5 = f32[8,16,1,128]{3,2,1,0:T(1,128)S(1)} fusion(f32[8,16,128,1]{2,3,1,0:T(1,128)S(1)} %bitcast.175, f32[8,16]{1,0:T(8,128)S(1)} %get-tuple-element.34, bf16[8,16,128,128]{3,2,1,0:T(8,128)(2,1)S(1)} %copy-done.1, f32[8,16,128]{2,1,0:T(8,128)S(1)} %subtract_multiply_fusion.1, f32[8,16,128]{2,1,0:T(8,128)S(1)} %bitcast.172, ...), kind=kOutput, calls=%fused_computation.14 | convolution fusion | flops 48234496 | bytes 4720640 | tf_op jit(solution)/shard_map/bhkv,bhk->bhv/dot_general | solution.py:46
  90.2 21.1 %fusion.10 = f32[8,16,1,128]{3,2,1,0:T(1,128)S(1)} fusion(f32[8,16,128,1]{2,3,1,0:T(1,128)S(1)} %bitcast.201, f32[8,16,128]{2,1,0:T(8,128)S(1)} %subtract_multiply_fusion, f32[8,16,128]{2,1,0:T(8,128)S(1)} %bitcast.176, f32[8,16]{1,0:T(8,128)S(1)} %get-tuple-element.34, bf16[8,16,128,128]{3,2,1,0:T(8,128)(2,1)S(1)} %copy-done.1, ...), kind=kOutput, calls=%fused_computation.19 | convolution fusion | flops 52428800 | bytes 4851712 | tf_op jit(solution)/shard_map/bhkv,bhk->bhv/dot_general | solution.py:51
  120.5 13.1 %all-to-all-done = bf16[8,32,2048]{2,1,0:T(8,128)(2,1)S(1)} async-done(((bf16[8,32,2048]{2,1,0:T(8,128)(2,1)}), bf16[8,32,2048]{2,1,0:T(8,128)(2,1)S(1)}, u32[]{:S(2)}, u32[]{:S(2)}) %all-to-all-start) | async-done | bytes 1048608 | tf_op jit(solution)/shard_map/all_to_all | solution.py:12
  140.2 5.3 all-to-all-done.1
  152.1 5.4 scatter_custom_fusion
  157.5 9.1 %reshape.507 = bf16[32,8,3,2048]{3,2,1,0:T(4,128)(2,1)} reshape(bf16[768,2048]{1,0:T(8,128)(2,1)} %scatter_custom_fusion) | data formatting | bytes 6291456 | tf_op jit(solution)/shard_map/reshape | solution.py:151
  166.6 5.5 copy.104
  172.1 84.1 %all_to_all.59 = bf16[32,8,3,2048]{3,1,2,0:T(8,128)(2,1)S(1)} all-to-all(bf16[32,8,3,2048]{3,1,2,0:T(8,128)(2,1)S(1)} %copy.104), channel_id=1, replica_groups=mesh['dp'=32,'ep'=8] {'dp'}, dimensions={0} | all-to-all | bytes 6291456 | tf_op jit(solution)/shard_map/all_to_all | solution.py:150
  259.6 4.6 all-to-all-start.3
  265.7 36.9 %all-to-all-done.3 = bf16[32,8,3,2048]{3,0,2,1:T(8,128)(2,1)} async-done(((bf16[32,8,3,2048]{3,0,2,1:T(8,128)(2,1)}), bf16[32,8,3,2048]{3,0,2,1:T(8,128)(2,1)}, u32[]{:S(2)}, u32[]{:S(2)}) %all-to-all-start.3) | async-done | bytes 3145760 | tf_op jit(solution)/shard_map/all_to_all | solution.py:149
  306.1 6.6 %copy.106 = bf16[32,8,3,2048]{3,2,1,0:T(4,128)(2,1)} copy(bf16[32,8,3,2048]{3,0,2,1:T(8,128)(2,1)} %all-to-all-done.3) | data formatting | bytes 6291456 | tf_op jit(solution)/shard_map/all_to_all | solution.py:149
  312.7 8.8 %reshape.508 = bf16[768,2048]{1,0:T(8,128)(2,1)} reshape(bf16[32,8,3,2048]{3,2,1,0:T(4,128)(2,1)} %copy.106) | data formatting | bytes 6291456 | tf_op jit(solution)/shard_map/reshape | solution.py:162
  328.0 9.1 %reshape.509 = bf16[32,8,3,2048]{3,2,1,0:T(4,128)(2,1)} reshape(bf16[768,2048]{1,0:T(8,128)(2,1)} %convolution_convert_fusion) | data formatting | bytes 6291456 | tf_op jit(solution)/shard_map/reshape | solution.py:162
  337.1 7.2 %copy.107 = bf16[32,8,3,2048]{3,1,2,0:T(8,128)(2,1)} copy(bf16[32,8,3,2048]{3,2,1,0:T(4,128)(2,1)} %reshape.509) | data formatting | bytes 6291456 | tf_op jit(solution)/shard_map/reshape | solution.py:162
  344.4 5.8 %all-to-all-start.4 = ((bf16[32,8,3,2048]{3,1,2,0:T(8,128)(2,1)}), bf16[32,8,3,2048]{3,1,2,0:T(8,128)(2,1)}, u32[]{:S(2)}, u32[]{:S(2)}) async-start(bf16[32,8,3,2048]{3,1,2,0:T(8,128)(2,1)} %copy.107), calls=%async_computation.4 | async-start | bytes 6291456 | tf_op jit(solution)/shard_map/all_to_all | solution.py:166
  350.3 13.3 %fusion.9 = bf16[8,16,128,128]{3,2,1,0:T(8,128)(2,1)} fusion(f32[8,16,128]{2,1,0:T(8,128)S(1)} %copy-done.14, f32[8,16,128]{2,1,0:T(8,128)S(1)} %bitcast.177, f32[8,16]{1,0:T(8,128)S(1)} %get-tuple-element.34, f32[8,16,128]{2,1,0:T(8,128)S(1)} %copy-done.12, f32[8,16,128]{2,1,0:T(8,128)S(1)} %bitcast.174, f32[8,16]{1,0:T(8,128)S(1)} %get-tuple-element.35, ...), kind=kLoop, calls=%fused_computation.18 | loop fusion | flops 29360128 | bytes 8914944 | tf_op jit(solution)/shard_map/convert_element_type | solution.py:60
  366.6 10.9 %scatter_fusion = bf16[8,16,128,128]{3,2,1,0:T(8,128)(2,1)} fusion(bf16[8,16,128,128]{3,2,1,0:T(8,128)(2,1)} %broadcast.334.clone, s32[8]{0:T(128)S(1)} %compare_select_fusion.2, bf16[8,16,128,128]{3,2,1,0:T(8,128)(2,1)} %fusion.9), kind=kCustom, calls=%fused_computation.3 | custom fusion | bytes 12582944 | tf_op jit(solution)/shard_map/scatter | solution.py:76
  377.4 46.9 %all-to-all-done.4 = bf16[32,8,3,2048]{3,1,2,0:T(8,128)(2,1)} async-done(((bf16[32,8,3,2048]{3,1,2,0:T(8,128)(2,1)}), bf16[32,8,3,2048]{3,1,2,0:T(8,128)(2,1)}, u32[]{:S(2)}, u32[]{:S(2)}) %all-to-all-start.4) | async-done | bytes 3145760 | tf_op jit(solution)/shard_map/all_to_all | solution.py:166
  424.3 4.8 all-to-all-start.7
  429.1 5.3 copy.108
  434.4 44.3 %all-to-all-done.7 = bf16[8,1,16,128,128]{4,3,2,1,0:T(8,128)(2,1)} async-done(((bf16[8,1,16,128,128]{4,3,2,1,0:T(8,128)(2,1)}), bf16[8,1,16,128,128]{4,3,2,1,0:T(8,128)(2,1)}, u32[]{:S(2)}, u32[]{:S(2)}) %all-to-all-start.7) | async-done | bytes 4194336 | tf_op jit(solution)/shard_map/all_to_all | solution.py:118
  487.4 10.9 %scatter_fusion.1 = bf16[8,16,128,128]{3,2,1,0:T(8,128)(2,1)} fusion(bf16[8,16,128,128]{3,2,1,0:T(8,128)(2,1)} %broadcast.334, s32[8]{0:T(128)S(1)} %fusion.54, bf16[8,16,128,128]{3,2,1,0:T(8,128)(2,1)} %bitcast.78), kind=kCustom, calls=%fused_computation.4 | custom fusion | bytes 12582944 | tf_op jit(solution)/shard_map/scatter | solution.py:125
  498.2 23.4 %all-to-all-done.5 = bf16[32,8,3,2048]{3,0,2,1:T(8,128)(2,1)} async-done(((bf16[32,8,3,2048]{3,0,2,1:T(8,128)(2,1)}), bf16[32,8,3,2048]{3,0,2,1:T(8,128)(2,1)}, u32[]{:S(2)}, u32[]{:S(2)}) %all-to-all-start.5) | async-done | bytes 3145760 | tf_op jit(solution)/shard_map/all_to_all | solution.py:165
  521.7 6.5 %copy.109 = bf16[32,8,3,2048]{3,2,1,0:T(4,128)(2,1)} copy(bf16[32,8,3,2048]{3,0,2,1:T(8,128)(2,1)} %all-to-all-done.5) | data formatting | bytes 6291456 | tf_op jit(solution)/shard_map/all_to_all | solution.py:165
  528.2 8.8 %reshape.510 = bf16[768,2048]{1,0:T(8,128)(2,1)} reshape(bf16[32,8,3,2048]{3,2,1,0:T(4,128)(2,1)} %copy.109) | data formatting | bytes 6291456 | tf_op jit(solution)/shard_map/reshape | solution.py:172
  537.0 6.8 %gather_fusion = bf16[320,2048]{1,0:T(8,128)(2,1)S(1)} fusion(bf16[768,2048]{1,0:T(8,128)(2,1)} %reshape.510, s32[1024]{0:T(1024)} %pad_clamp_fusion), kind=kCustom, calls=%fused_computation | custom fusion | bytes 2622720 | tf_op jit(solution)/shard_map/gather | solution.py:172
  (171 shorter events, 63.1 us)
Async XLA Ops:
  0.6 320.9 %copy-start = (bf16[1,2048,512]{2,1,0:T(8,128)(2,1)S(1)}, bf16[1,2048,512]{2,1,0:T(8,128)(2,1)}, u32[]{:S(2)}) copy-start(bf16[1,2048,512]{2,1,0:T(8,128)(2,1)} %param.29) | copy-start | bytes 6291460
  2.4 15.1 %copy-start.1 = (bf16[8,16,128,128]{3,2,1,0:T(8,128)(2,1)S(1)}, bf16[8,16,128,128]{3,2,1,0:T(8,128)(2,1)}, u32[]{:S(2)}) copy-start(bf16[8,16,128,128]{3,2,1,0:T(8,128)(2,1)} %param.16) | copy-start | bytes 12582916
  7.7 82.4 %copy-start.15 = (f32[8,8,2,128]{3,2,1,0:T(2,128)}, f32[8,8,2,128]{3,2,1,0:T(2,128)S(1)}, u32[]{:S(2)}) copy-start(f32[8,8,2,128]{3,2,1,0:T(2,128)S(1)} %broadcast_in_dim.22) | copy-start | bytes 196612
  17.5 72.6 %copy-start.7 = (f32[8,16,128]{2,1,0:T(8,128)}, f32[8,16,128]{2,1,0:T(8,128)S(1)}, u32[]{:S(2)}) copy-start(f32[8,16,128]{2,1,0:T(8,128)S(1)} %subtract_multiply_fusion.3) | copy-start | bytes 196612
  26.0 64.1 %copy-start.17 = (f32[8,8,2,128]{3,2,1,0:T(2,128)}, f32[8,8,2,128]{3,2,1,0:T(2,128)S(1)}, u32[]{:S(2)}) copy-start(f32[8,8,2,128]{3,2,1,0:T(2,128)S(1)} %broadcast_in_dim.24) | copy-start | bytes 196612
  35.1 55.1 %copy-start.9 = (f32[8,16,128]{2,1,0:T(8,128)}, f32[8,16,128]{2,1,0:T(8,128)S(1)}, u32[]{:S(2)}) copy-start(f32[8,16,128]{2,1,0:T(8,128)S(1)} %subtract_multiply_fusion.2) | copy-start | bytes 196612
  46.9 43.3 %copy-start.19 = (f32[8,8,2,128]{3,2,1,0:T(2,128)}, f32[8,8,2,128]{3,2,1,0:T(2,128)S(1)}, u32[]{:S(2)}) copy-start(f32[8,8,2,128]{3,2,1,0:T(2,128)S(1)} %broadcast_in_dim.26) | copy-start | bytes 196612
  58.6 31.5 %copy-start.11 = (f32[8,16,128]{2,1,0:T(8,128)}, f32[8,16,128]{2,1,0:T(8,128)S(1)}, u32[]{:S(2)}) copy-start(f32[8,16,128]{2,1,0:T(8,128)S(1)} %subtract_multiply_fusion.1) | copy-start | bytes 196612
  74.3 15.8 %copy-start.21 = (f32[8,8,2,128]{3,2,1,0:T(2,128)}, f32[8,8,2,128]{3,2,1,0:T(2,128)S(1)}, u32[]{:S(2)}) copy-start(f32[8,8,2,128]{3,2,1,0:T(2,128)S(1)} %broadcast_in_dim.28) | copy-start | bytes 196612
  90.1 21.3 %copy-start.13 = (f32[8,16,128]{2,1,0:T(8,128)}, f32[8,16,128]{2,1,0:T(8,128)S(1)}, u32[]{:S(2)}) copy-start(f32[8,16,128]{2,1,0:T(8,128)S(1)} %subtract_multiply_fusion) | copy-start | bytes 196612
  90.2 21.3 %copy-start.6 = (bf16[8,4,2048]{2,1,0:T(4,128)(2,1)S(1)}, bf16[8,4,2048]{2,1,0:T(4,128)(2,1)}, u32[]{:S(2)}) copy-start(bf16[8,4,2048]{2,1,0:T(4,128)(2,1)} %param.20) | copy-start | bytes 393220
  90.2 21.5 %copy-start.26 = (f32[128]{0:T(128)S(1)}, f32[128]{0:T(128)}, u32[]{:S(2)}) copy-start(f32[128]{0:T(128)} %param.27) | copy-start | bytes 1540
  111.3 6.3 %copy-start.23 = (s32[8,4,10]{2,1,0:T(4,128)S(1)}, s32[8,4,10]{2,1,0:T(4,128)}, u32[]{:S(2)}) copy-start(s32[8,4,10]{2,1,0:T(4,128)} %param.24) | copy-start | bytes 3844
  113.2 26.4 %copy-start.5 = (bf16[8,4,2048]{2,1,0:T(4,128)(2,1)S(1)}, bf16[8,4,2048]{2,1,0:T(4,128)(2,1)}, u32[]{:S(2)}) copy-start(bf16[8,4,2048]{2,1,0:T(4,128)(2,1)} %param.23) | copy-start | bytes 393220
  113.2 20.4 %all-to-all-start = ((bf16[8,32,2048]{2,1,0:T(8,128)(2,1)}), bf16[8,32,2048]{2,1,0:T(8,128)(2,1)S(1)}, u32[]{:S(2)}, u32[]{:S(2)}) async-start(bf16[8,32,2048]{2,1,0:T(8,128)(2,1)} %tile.9), calls=%async_computation | async-start | bytes 2097152 | tf_op jit(solution)/shard_map/all_to_all | solution.py:12
  135.9 9.6 %all-to-all-start.1 = ((bf16[8,32,256]{2,1,0:T(8,128)(2,1)}), bf16[8,32,256]{2,1,0:T(8,128)(2,1)S(1)}, u32[]{:S(2)}, u32[]{:S(2)}) async-start(bf16[8,32,256]{2,1,0:T(8,128)(2,1)} %bitcast.65), calls=%async_computation.1 | async-start | bytes 262144 | tf_op jit(solution)/shard_map/all_to_all | solution.py:131
  145.9 11.7 %copy-start.2 = (f32[8,4,2048]{2,1,0:T(4,128)}, f32[8,4,2048]{2,1,0:T(4,128)S(1)}, u32[]{:S(2)}) copy-start(f32[8,4,2048]{2,1,0:T(4,128)S(1)} %reshape.546) | copy-start | bytes 786436
  259.6 43.0 %all-to-all-start.3 = ((bf16[32,8,3,2048]{3,0,2,1:T(8,128)(2,1)}), bf16[32,8,3,2048]{3,0,2,1:T(8,128)(2,1)}, u32[]{:S(2)}, u32[]{:S(2)}) async-start(bf16[32,8,3,2048]{3,0,2,1:T(8,128)(2,1)} %copy.105), calls=%async_computation.3 | async-start | bytes 6291456 | tf_op jit(solution)/shard_map/all_to_all | solution.py:149
  302.6 41.8 %all-to-all-start.6 = ((s32[8,1,1]{2,1,0:T(1,128)}), s32[8,1,1]{2,1,0:T(1,128)S(1)}, u32[]{:S(2)}, u32[]{:S(2)}) async-start(s32[8,1,1]{2,1,0:T(1,128)} %copy.110), calls=%async_computation.6 | async-start | bytes 8192 | tf_op jit(solution)/shard_map/all_to_all | solution.py:121
  344.3 5.8 %copy-start.8 = (f32[8,16,128]{2,1,0:T(8,128)S(1)}, f32[8,16,128]{2,1,0:T(8,128)}, u32[]{:S(2)}) copy-start(f32[8,16,128]{2,1,0:T(8,128)} %copy-done.7) | copy-start | bytes 196612
  344.3 5.8 %copy-start.10 = (f32[8,16,128]{2,1,0:T(8,128)S(1)}, f32[8,16,128]{2,1,0:T(8,128)}, u32[]{:S(2)}) copy-start(f32[8,16,128]{2,1,0:T(8,128)} %copy-done.9) | copy-start | bytes 196612
  344.3 5.8 %copy-start.12 = (f32[8,16,128]{2,1,0:T(8,128)S(1)}, f32[8,16,128]{2,1,0:T(8,128)}, u32[]{:S(2)}) copy-start(f32[8,16,128]{2,1,0:T(8,128)} %copy-done.11) | copy-start | bytes 196612
  344.4 5.9 %copy-start.14 = (f32[8,16,128]{2,1,0:T(8,128)S(1)}, f32[8,16,128]{2,1,0:T(8,128)}, u32[]{:S(2)}) copy-start(f32[8,16,128]{2,1,0:T(8,128)} %copy-done.13) | copy-start | bytes 196612
  344.4 5.9 %copy-start.16 = (f32[8,8,2,128]{3,2,1,0:T(2,128)S(1)}, f32[8,8,2,128]{3,2,1,0:T(2,128)}, u32[]{:S(2)}) copy-start(f32[8,8,2,128]{3,2,1,0:T(2,128)} %copy-done.15) | copy-start | bytes 196612
  344.4 5.9 %copy-start.18 = (f32[8,8,2,128]{3,2,1,0:T(2,128)S(1)}, f32[8,8,2,128]{3,2,1,0:T(2,128)}, u32[]{:S(2)}) copy-start(f32[8,8,2,128]{3,2,1,0:T(2,128)} %copy-done.17) | copy-start | bytes 196612
  344.4 5.9 %copy-start.20 = (f32[8,8,2,128]{3,2,1,0:T(2,128)S(1)}, f32[8,8,2,128]{3,2,1,0:T(2,128)}, u32[]{:S(2)}) copy-start(f32[8,8,2,128]{3,2,1,0:T(2,128)} %copy-done.19) | copy-start | bytes 196612
  344.4 5.9 %copy-start.22 = (f32[8,8,2,128]{3,2,1,0:T(2,128)S(1)}, f32[8,8,2,128]{3,2,1,0:T(2,128)}, u32[]{:S(2)}) copy-start(f32[8,8,2,128]{3,2,1,0:T(2,128)} %copy-done.21) | copy-start | bytes 196612
  344.4 79.9 %all-to-all-start.4 = ((bf16[32,8,3,2048]{3,1,2,0:T(8,128)(2,1)}), bf16[32,8,3,2048]{3,1,2,0:T(8,128)(2,1)}, u32[]{:S(2)}, u32[]{:S(2)}) async-start(bf16[32,8,3,2048]{3,1,2,0:T(8,128)(2,1)} %copy.107), calls=%async_computation.4 | async-start | bytes 6291456 | tf_op jit(solution)/shard_map/all_to_all | solution.py:166
  424.3 54.5 %all-to-all-start.7 = ((bf16[8,1,16,128,128]{4,3,2,1,0:T(8,128)(2,1)}), bf16[8,1,16,128,128]{4,3,2,1,0:T(8,128)(2,1)}, u32[]{:S(2)}, u32[]{:S(2)}) async-start(bf16[8,1,16,128,128]{4,3,2,1,0:T(8,128)(2,1)} %bitcast.133), calls=%async_computation.7 | async-start | bytes 8388608 | tf_op jit(solution)/shard_map/all_to_all | solution.py:118
  434.4 48.8 %copy-start.24 = (f32[8,4,10]{2,1,0:T(4,128)S(1)}, f32[8,4,10]{2,1,0:T(4,128)}, u32[]{:S(2)}) copy-start(f32[8,4,10]{2,1,0:T(4,128)} %param.25) | copy-start | bytes 3844
  434.4 49.0 %copy-start.25 = (s32[320]{0:T(512)S(1)}, s32[320]{0:T(512)}, u32[]{:S(2)}) copy-start(s32[320]{0:T(512)} %fusion.52) | copy-start | bytes 3844
  478.8 42.9 %all-to-all-start.5 = ((bf16[32,8,3,2048]{3,0,2,1:T(8,128)(2,1)}), bf16[32,8,3,2048]{3,0,2,1:T(8,128)(2,1)}, u32[]{:S(2)}, u32[]{:S(2)}) async-start(bf16[32,8,3,2048]{3,0,2,1:T(8,128)(2,1)} %copy.108), calls=%async_computation.5 | async-start | bytes 6291456 | tf_op jit(solution)/shard_map/all_to_all | solution.py:165
  (4 other events, 12.9 us)
